TPU v7x, 512 devices: a whole 4x8x8 slice. The times are simulated.
512 devices in a mesh: ctx: 32 (over z, x), ch: 16 (over y, core).
Axes of the slice: x: 4, y: 8, z: 8, core: 2. Of those that a mesh axis runs over, the one named last changes fastest.
Arguments:
- query_seq: bfloat16 [4096, 4096], P('ctx', 'ch'), may hold values from -6 to 6
- key_seq: bfloat16 [4096, 4096], P('ctx', 'ch'), may hold values from -6 to 6
- value_seq: bfloat16 [4096, 4096], P('ctx', 'ch'), may hold values from -6 to 6
- out_grad: bfloat16 [4096, 4096], P('ctx', 'ch'), may hold values from -6 to 6
- filters: bfloat16 [4096, 256], P('ctx', 'ch'), may hold values from -6 to 6
- skip_gain: float32 [4096], P('ch'), may hold values from -1 to 1
- reaches: int32 [256], P('ch'), may hold values from 1 to 32, as said below
Outputs:
- mixed: bfloat16 [4096, 4096], P('ctx', 'ch')
- query_grad: bfloat16 [4096, 4096], P('ctx', 'ch')
- key_grad: bfloat16 [4096, 4096], P('ctx', 'ch')
- value_grad: bfloat16 [4096, 4096], P('ctx', 'ch')
- filter_grad: float32 [4096, 256], P('ctx', 'ch')
- skip_grad: float32 [4096], P('ch')
Inputs may be any that keep to these rules, and one draw needn't show every extreme that they name: Each group's reach counts its own span; some group reaches the whole context and some group only its own span.
All inputs are finite; a program needn't handle non-finite values.
Results may differ from a plain program's by a relative error of at most 0.01.
Values may be sent and summed in bfloat16 or wider, within the bound.
No kernel may reach another device: no remote copies, remote signals or barrier semaphores. Data moves between devices by JAX's collectives and lax.ppermute only.
A program may use at most 64 MiB of HBM per device.

v0:
```python
import math
import jax
import jax.numpy as jnp
from jax import lax
from jax.sharding import PartitionSpec as P

GROUP = 16


def toeplitz(window):
    size_two, groups = window.shape
    block_len = size_two // 2
    flipped = window[::-1].T
    tiled = jnp.tile(flipped, (1, block_len))
    shaped = tiled[:, : block_len * (2 * block_len - 1)].reshape(
        groups, block_len, 2 * block_len - 1
    )
    return shaped[:, :, block_len - 1 :]


def diag_sum(prods):
    groups, block_len, _ = prods.shape
    padded = jnp.pad(prods, ((0, 0), (0, 0), (block_len - 1, 0)))
    flat = padded.reshape(groups, block_len * (2 * block_len - 1))
    flat = jnp.pad(flat, ((0, 0), (0, block_len)))
    sums = flat.reshape(groups, block_len, 2 * block_len).sum(axis=1)
    return sums[:, ::-1].T


def add_window(tap_sums, window_grad, offset, block_len):
    current = lax.dynamic_slice_in_dim(tap_sums, offset * block_len, 2 * block_len, 0)
    return lax.dynamic_update_slice_in_dim(tap_sums, current + window_grad, offset * block_len, 0)


def kernel_block(taps, limits, offset, block_len):
    window = lax.dynamic_slice_in_dim(taps, offset * block_len, 2 * block_len, 0)
    weights = offset < limits
    tmat = toeplitz(window) * weights.astype(jnp.bfloat16)[:, None, None]
    return (tmat, weights.astype(jnp.float32))


def body(query_seq, key_seq, value_seq, out_grad, filters, skip_gain, reaches):
    f32 = jnp.float32
    block_len = query_seq.shape[0]
    local_width = query_seq.shape[1]
    local_groups = local_width // GROUP
    num_spans = lax.axis_size("ctx")
    seq_len = block_len * num_spans
    scale = 1.0 / math.sqrt(seq_len)
    myself = lax.axis_index("ctx")
    z_vals = (key_seq.astype(f32) * value_seq.astype(f32)).astype(jnp.bfloat16)
    grads = (out_grad.astype(f32) * query_seq.astype(f32)).astype(jnp.bfloat16)
    all_taps = lax.all_gather(filters, "ctx", axis=0, tiled=True)
    taps = jnp.concatenate([jnp.zeros((block_len, local_groups), jnp.bfloat16), all_taps], axis=0)
    longest = jnp.max(reaches)
    own_grads = grads.reshape(block_len, local_groups, GROUP)
    start = (
        jnp.zeros((block_len, local_groups, GROUP), f32),
        jnp.zeros((block_len, local_groups, GROUP), f32),
        jnp.zeros((seq_len + block_len, local_groups), f32),
    )
    z_piece = lax.all_gather(z_vals, "ctx", axis=0, tiled=True)
    g_piece = lax.all_gather(grads, "ctx", axis=0, tiled=True)
    count = z_piece.shape[0] // block_len

    def span_step(position, state):
        filtered, back_sum, tap_sums = state
        remote_z = lax.dynamic_slice_in_dim(z_piece, position * block_len, block_len, 0)
        remote_z = remote_z.reshape(block_len, local_groups, GROUP)
        remote_g = lax.dynamic_slice_in_dim(g_piece, position * block_len, block_len, 0)
        remote_g = remote_g.reshape(block_len, local_groups, GROUP)
        ahead = myself - position
        behind = position - myself

        def forward(inner):
            acc, sums = inner
            tmat, weights = kernel_block(taps, reaches, ahead, block_len)
            acc = acc + jnp.einsum("gab,bgc->agc", tmat, remote_z, preferred_element_type=f32)
            prods = jnp.einsum("agc,bgc->gab", own_grads, remote_z, preferred_element_type=f32)
            prods = prods * weights[:, None, None]
            return (acc, add_window(sums, diag_sum(prods), ahead, block_len))

        filtered, tap_sums = lax.cond(
            (ahead >= 0) & (ahead < longest), forward, lambda inner: inner, (filtered, tap_sums)
        )

        def backward(acc):
            tmat, weights = kernel_block(taps, reaches, behind, block_len)
            return acc + jnp.einsum("gab,agc->bgc", tmat, remote_g, preferred_element_type=f32)

        back_sum = lax.cond((behind >= 0) & (behind < longest), backward, lambda acc: acc, back_sum)
        return (filtered, back_sum, tap_sums)

    filtered, back_sum, tap_sums = lax.fori_loop(0, count, span_step, start)
    filtered = filtered.reshape(block_len, local_width)
    back_sum = back_sum.reshape(block_len, local_width)
    filter_grad = (
        lax.psum_scatter(tap_sums[block_len:], "ctx", scatter_dimension=0, tiled=True) * scale
    )
    skip_grad = lax.psum(jnp.sum(grads.astype(f32) * z_vals.astype(f32), axis=0), "ctx")
    filtered = filtered * scale
    back_sum = back_sum * scale
    total = filtered + skip_gain[None, :] * z_vals.astype(f32)
    mixed = (query_seq.astype(f32) * total).astype(jnp.bfloat16)
    query_grad = (out_grad.astype(f32) * total).astype(jnp.bfloat16)
    back_total = back_sum + skip_gain[None, :] * grads.astype(f32)
    key_grad = (back_total * value_seq.astype(f32)).astype(jnp.bfloat16)
    value_grad = (back_total * key_seq.astype(f32)).astype(jnp.bfloat16)
    return (mixed, query_grad, key_grad, value_grad, filter_grad, skip_grad)


def solution(mesh):
    in_specs = (
        P("ctx", "ch"),
        P("ctx", "ch"),
        P("ctx", "ch"),
        P("ctx", "ch"),
        P("ctx", "ch"),
        P("ch"),
        P("ch"),
    )
    out_specs = (
        P("ctx", "ch"),
        P("ctx", "ch"),
        P("ctx", "ch"),
        P("ctx", "ch"),
        P("ctx", "ch"),
        P("ch"),
    )
    return jax.shard_map(body, mesh=mesh, in_specs=in_specs, out_specs=out_specs, check_vma=False)
```

profile of v0, /device:TPU:8, one launch (start us, length us, event | category | flops | bytes accessed | tf_op | source)
XLA Modules:
  0.0 960.7 jit_solution(9368183063505255978)
XLA Ops:
  14.0 55.2 %all_gather.9 = bf16[4096,16]{0,1:T(8,128)(2,1)S(1)} all-gather(bf16[128,16]{0,1:T(8,128)(2,1)} %param.17), channel_id=1, replica_groups=mesh['ctx'=32,'ch'=16] {'ctx'}, dimensions={0}, use_global_device_ids=true | all-gather | bytes 135168 | tf_op jit(solution)/shard_map/all_gather | solution.py:53
  69.9 28.0 %all-gather.3.cloned.1.call-done = bf16[4096,256]{0,1:T(8,128)(2,1)} async-done(((bf16[128,256]{0,1:T(8,128)(2,1)}), bf16[4096,256]{0,1:T(8,128)(2,1)}) %all-gather.3.cloned.1.call-update) | async-done | bytes 2097168 | tf_op jit(solution)/shard_map/all_gather | solution.py:62
  97.9 83.6 %all-gather.5.cloned.1.call-done = bf16[4096,256]{0,1:T(8,128)(2,1)} async-done(((bf16[128,256]{0,1:T(8,128)(2,1)}), bf16[4096,256]{0,1:T(8,128)(2,1)}) %all-gather.5.cloned.1.call-update) | async-done | bytes 2097168 | tf_op jit(solution)/shard_map/all_gather | solution.py:63
  182.2 303.9 %while.20 = (s32[]{:T(128)}, f32[128,16,16]{0,2,1:T(8,128)S(1)}, f32[128,16,16]{0,2,1:T(8,128)}, f32[4224,16]{0,1:T(8,128)S(1)}, s32[]{:T(128)}, /*index=5*/s32[...) while((s32[]{:T(128)}, f32[128,16,16]{0,2,1:T(8,128)S(1)}, ...), condition=%wide.region_7.8_spmd, body=%wide.region_1.7_spmd.sunk | while | flops 27328612 | bytes 39176128 | solution.py:94
  183.5 8.4 conditional.5
  192.0 15.6 %conditional.4 = ((f32[128,16,16]{0,2,1:T(8,128)S(1)}, f32[4224,16]{0,1:T(8,128)S(1)})) conditional(s32[]{:T(128)} %convert_element_type.145, (f32[128,16,16]{0,2,1:T(8,128)S(1)}, f32[4224,16]{0,1:T(8,128)S(1)}) %tuple.66, (s32[]{:T(128)}, bf16[4224,16]{0,1:T(8,128)(2,1)}, s32[16]{0:T(128)}, bf16[4096,256]{0,1:T(8,128)(2,1)}, s32[]{:T(128)}, ...), branch_computations={%region_2.0_spmd, %region_3.4_spmd} | conditional | flops 17858612 | bytes 30565238 | solution.py:83
  208.8 8.4 conditional.5
  218.6 8.4 conditional.5
  228.3 8.4 conditional.5
  238.0 8.4 conditional.5
  247.7 8.4 conditional.5
  257.4 8.4 conditional.5
  267.2 8.4 conditional.5
  276.9 8.4 conditional.5
  286.6 8.4 conditional.5
  296.3 8.4 conditional.5
  306.1 8.4 conditional.5
  315.8 8.4 conditional.5
  325.5 8.4 conditional.5
  335.2 8.4 conditional.5
  345.0 8.4 conditional.5
  354.7 8.4 conditional.5
  364.4 8.4 conditional.5
  374.1 8.4 conditional.5
  383.8 8.4 conditional.5
  393.6 8.4 conditional.5
  403.3 8.4 conditional.5
  413.0 8.4 conditional.5
  432.5 8.4 conditional.5
  461.6 8.4 conditional.5
  486.9 311.9 %psum.7 = f32[256]{0:T(256)} all-reduce(f32[256]{0:T(256)S(1)} %get-tuple-element.328), channel_id=1, replica_groups=mesh['ctx'=32,'ch'=16] {'ctx'}, use_global_device_ids=true, to_apply=%region_10.11 | all-reduce | flops 256 | bytes 2048 | tf_op jit(solution)/shard_map/psum | solution.py:100
  803.8 149.0 %reduce-scatter.2.cloned.1.call-done = f32[128,16]{0,1:T(8,128)} async-done(((f32[4096,16]{0,1:T(8,128)}), f32[128,16]{0,1:T(8,128)}) %reduce-scatter.2.cloned.1.call-update) | async-done | bytes 8208 | tf_op jit(solution)/shard_map/reduce_scatter | solution.py:98
  (419 shorter events, 311.0 us)
Async XLA Ops:
  7.2 90.8 %all-gather.3.cloned.1.call-start = ((), (), s32[]{:S(2)}) async-start(), calls=%async_computation.1 | async-start | bytes 2162688 | tf_op jit(solution)/shard_map/all_gather | solution.py:62
  8.2 174.0 %copy-start.1 = (bf16[128,256]{0,1:T(8,128)(2,1)}, bf16[128,256]{0,1:T(8,128)(2,1)S(1)}, u32[]{:S(2)}) copy-start(bf16[128,256]{0,1:T(8,128)(2,1)S(1)} %copy.19) | copy-start | bytes 196612
  9.2 173.0 %copy-start.2 = (bf16[128,256]{0,1:T(8,128)(2,1)}, bf16[128,256]{0,1:T(8,128)(2,1)S(1)}, u32[]{:S(2)}) copy-start(bf16[128,256]{0,1:T(8,128)(2,1)S(1)} %copy.20) | copy-start | bytes 196612
  10.2 172.0 %copy-start.3 = (bf16[128,256]{0,1:T(8,128)(2,1)}, bf16[128,256]{0,1:T(8,128)(2,1)S(1)}, u32[]{:S(2)}) copy-start(bf16[128,256]{0,1:T(8,128)(2,1)S(1)} %copy.21) | copy-start | bytes 196612
  11.1 171.0 %copy-start.4 = (bf16[128,256]{0,1:T(8,128)(2,1)}, bf16[128,256]{0,1:T(8,128)(2,1)S(1)}, u32[]{:S(2)}) copy-start(bf16[128,256]{0,1:T(8,128)(2,1)S(1)} %copy.22) | copy-start | bytes 196612
  11.9 169.6 %all-gather.5.cloned.1.call-start = ((), (), s32[]{:S(2)}) async-start(), calls=%async_computation.2 | async-start | bytes 2162688 | tf_op jit(solution)/shard_map/all_gather | solution.py:63
  12.6 940.2 %reduce-scatter.2.cloned.1.call-start = ((), (), s32[]{:S(2)}) async-start(), calls=%async_computation.3 | async-start | bytes 270336 | tf_op jit(solution)/shard_map/reduce_scatter | solution.py:98
  182.2 617.4 %copy-start.7 = (f32[256]{0:T(256)S(1)}, f32[256]{0:T(256)}, u32[]{:S(2)}) copy-start(f32[256]{0:T(256)} %param.18) | copy-start | bytes 3076
  183.5 8.5 copy-start
  208.8 8.5 copy-start
  218.5 8.5 copy-start
  228.3 8.5 copy-start
  238.0 8.5 copy-start
  247.7 8.5 copy-start
  257.4 8.5 copy-start
  267.2 8.5 copy-start
  276.9 8.5 copy-start
  296.3 8.5 copy-start
  306.1 8.5 copy-start
  315.8 8.5 copy-start
  325.5 8.5 copy-start
  335.2 8.5 copy-start
  344.9 8.5 copy-start
  364.4 8.5 copy-start
  374.1 8.5 copy-start
  383.8 8.5 copy-start
  393.6 8.5 copy-start
  403.3 8.5 copy-start
  413.0 8.5 copy-start
  422.7 8.5 copy-start
  432.4 8.5 copy-start
  461.6 8.5 copy-start
  (10 other events, 48.1 us)
Sparse Core Ops, SparseCore 0:
  12.0 85.8 all-gather.2
  101.6 79.9 all-gather.4
  487.0 465.8 reduce-scatter.1
where the time goes:
time: 969 us; the launch traced here: 961 us
  blocking collectives  367 us (38%)
  waiting for transfers between devices  261 us (27%)
  local copies, waits for them, and re-layouts  193 us (20%)
  matrix products  58 us (6%)
  loops' own time  42 us (4%)
  other arithmetic  25.4 us (3%)
  between operations  13.9 us (1%)
    psum x1, blocking collectives, body(): lax.psum(jnp.sum(grads.astype(f32) * z_vals.astype(f32), axis=0), 'ctx')  312 us
    reduce_scatter x1, waiting for transfers between devices, body(): lax.psum_scatter(tap_sums[block_len:], 'ctx', scatter_dimension=0, tiled=...  149 us
    reshape x30, local copies, waits for them, and re-layouts, toeplitz(): tiled[:, :block_len * (2 * block_len - 1)]  102 us
    all_gather x1, waiting for transfers between devices, body(): g_piece = lax.all_gather(grads, 'ctx', axis=0, tiled=True)  83.6 us
    dot_general x29, matrix products, backward(): jnp.einsum('gab,agc->bgc', tmat, remote_g, preferred_element_type=f32)  55.6 us
    all_gather x1, blocking collectives, body(): all_taps = lax.all_gather(filters, 'ctx', axis=0, tiled=True)  55.2 us
    another operation x1, loops' own time, body(): filtered, back_sum, tap_sums = lax.fori_loop(0, count, span_step, start)  40.6 us
    all_gather x1, waiting for transfers between devices, body(): z_piece = lax.all_gather(z_vals, 'ctx', axis=0, tiled=True)  28 us
  transfers between devices with their start and end apart: 3, of which 3 were waited for; matrix products, arithmetic and copies ran while one was open for 1% of the time, Pallas kernels for 0%

commit v1 on v0

--- a/solution.py
+++ b/solution.py
@@ -59,8 +59,12 @@
         jnp.zeros((block_len, local_groups, GROUP), f32),
         jnp.zeros((seq_len + block_len, local_groups), f32),
     )
-    z_piece = lax.all_gather(z_vals, "ctx", axis=0, tiled=True)
-    g_piece = lax.all_gather(grads, "ctx", axis=0, tiled=True)
+    replace_the_face = lambda load, unit, row_axis: jnp.split(
+        lax.all_gather(jnp.concatenate([load, unit], axis=1), row_axis, axis=0, tiled=True),
+        [load.shape[1]],
+        axis=1,
+    )
+    z_piece, g_piece = replace_the_face(z_vals, grads, "ctx")
     count = z_piece.shape[0] // block_len
 
     def span_step(position, state):

time: 969 us -> 856 us (0.88)
  waiting for transfers between devices: 261 us -> 185 us
  other arithmetic: 25.4 us -> 5.7 us
  blocking collectives: 367 us -> 348 us
    all_gather x2 -> x1, waiting for transfers between devices: 112 us -> 36.6 us  [body(): lax.all_gather(jnp.concatenate([load, unit], axis=1), row_axis, axis=0, t...]
    psum x1, blocking collectives: 312 us -> 293 us  [body(): lax.psum(jnp.sum(grads.astype(f32) * z_vals.astype(f32), axis=0), 'ctx')]
    convert_element_type x29, other arithmetic: 19.2 us -> 0.14 us  [kernel_block(): tmat = toeplitz(window) * weights.astype(jnp.bfloat16)[:, None, None]]
  transfers between devices with their start and end apart: 3 -> 2, of which waited for: 3 -> 2; matrix products, arithmetic and copies ran while one was open for 1% -> 1% of each run, Pallas kernels for 0% -> 0%
where the time goes in v1:
time: 856 us; the launch traced here: 849 us
  blocking collectives  348 us (41%)
  local copies, waits for them, and re-layouts  196 us (23%)
  waiting for transfers between devices  185 us (22%)
  matrix products  58 us (7%)
  loops' own time  42.6 us (5%)
  between operations  14.2 us (2%)
    psum x1, blocking collectives, body(): lax.psum(jnp.sum(grads.astype(f32) * z_vals.astype(f32), axis=0), 'ctx')  293 us
    reduce_scatter x1, waiting for transfers between devices, body(): lax.psum_scatter(tap_sums[block_len:], 'ctx', scatter_dimension=0, tiled=...  148 us
    reshape x30, local copies, waits for them, and re-layouts, toeplitz(): tiled[:, :block_len * (2 * block_len - 1)]  102 us
    dot_general x29, matrix products, backward(): jnp.einsum('gab,agc->bgc', tmat, remote_g, preferred_element_type=f32)  55.6 us
    all_gather x1, blocking collectives, body(): all_taps = lax.all_gather(filters, 'ctx', axis=0, tiled=True)  55.3 us
    another operation x1, loops' own time, body(): filtered, back_sum, tap_sums = lax.fori_loop(0, count, span_step, start)  41 us
    all_gather x1, waiting for transfers between devices, body(): lax.all_gather(jnp.concatenate([load, unit], axis=1), row_axis, axis=0, t...  36.6 us
    dynamic_slice x29, local copies, waits for them, and re-layouts, span_step(): lax.dynamic_slice_in_dim(g_piece, position * block_len, block_len, 0)  24.5 us
  transfers between devices with their start and end apart: 2, of which 2 were waited for; matrix products, arithmetic and copies ran while one was open for 1% of the time, Pallas kernels for 0%

profile of v1, /device:TPU:8, one launch (start us, length us, event | category | flops | bytes accessed | tf_op | source)
XLA Modules:
  0.0 849.1 jit_solution(16423132895359161047)
XLA Ops:
  14.0 55.3 %all_gather.6 = bf16[4096,16]{0,1:T(8,128)(2,1)S(1)} all-gather(bf16[128,16]{0,1:T(8,128)(2,1)} %param.17), channel_id=1, replica_groups=mesh['ctx'=32,'ch'=16] {'ctx'}, dimensions={0}, use_global_device_ids=true | all-gather | bytes 135168 | tf_op jit(solution)/shard_map/all_gather | solution.py:53
  69.9 36.6 %all-gather.2.cloned.1.call-done = bf16[4096,512]{0,1:T(8,128)(2,1)} async-done(((bf16[128,512]{0,1:T(8,128)(2,1)}), bf16[4096,512]{0,1:T(8,128)(2,1)}) %all-gather.2.cloned.1.call-update) | async-done | bytes 4194320 | tf_op jit(solution)/shard_map/all_gather | solution.py:63
  111.9 282.6 %while.20 = (s32[]{:T(128)}, f32[128,16,16]{0,2,1:T(8,128)S(1)}, f32[128,16,16]{0,2,1:T(8,128)}, f32[4224,16]{0,1:T(8,128)S(1)}, s32[]{:T(128)}, /*index=5*/s32[...) while((s32[]{:T(128)}, f32[128,16,16]{0,2,1:T(8,128)S(1)}, ...), condition=%wide.region_7.8_spmd, body=%wide.region_1.7_spmd.sunk | while | flops 27328612 | bytes 38913960 | solution.py:98
  113.2 7.8 conditional.5
  121.0 15.0 %conditional.4 = ((f32[128,16,16]{0,2,1:T(8,128)S(1)}, f32[4224,16]{0,1:T(8,128)S(1)})) conditional(s32[]{:T(128)} %convert_element_type.145, (f32[128,16,16]{0,2,1:T(8,128)S(1)}, f32[4224,16]{0,1:T(8,128)S(1)}) %tuple.67, (s32[]{:T(128)}, bf16[4224,16]{0,1:T(8,128)(2,1)}, s32[16]{0:T(128)S(1)}, bf16[4096,256]{0,1:T(8,128)(2,1)}, s32[]{:T(128)}, ...), branch_computations={%region_2.0_spmd, %region_3.4_spmd} | conditional | flops 17858612 | bytes 30565238 | solution.py:87
  137.2 7.8 conditional.5
  146.3 7.8 conditional.5
  155.4 7.8 conditional.5
  164.5 7.8 conditional.5
  173.6 7.8 conditional.5
  182.7 7.8 conditional.5
  191.8 7.8 conditional.5
  200.9 7.8 conditional.5
  210.0 7.8 conditional.5
  219.0 7.8 conditional.5
  228.1 7.8 conditional.5
  237.2 7.8 conditional.5
  246.3 7.8 conditional.5
  255.4 7.8 conditional.5
  264.5 7.8 conditional.5
  273.6 7.8 conditional.5
  282.7 7.8 conditional.5
  291.7 7.8 conditional.5
  300.8 7.8 conditional.5
  309.9 7.8 conditional.5
  319.0 7.8 conditional.5
  328.1 7.8 conditional.5
  346.3 7.8 conditional.5
  373.5 7.8 conditional.5
  382.6 7.8 conditional.5
  395.2 292.8 %psum.7 = f32[256]{0:T(256)} all-reduce(f32[256]{0:T(256)S(1)} %get-tuple-element.328), channel_id=1, replica_groups=mesh['ctx'=32,'ch'=16] {'ctx'}, use_global_device_ids=true, to_apply=%region_10.11 | all-reduce | flops 256 | bytes 2048 | tf_op jit(solution)/shard_map/psum | solution.py:104
  693.0 148.0 %reduce-scatter.2.cloned.1.call-done = f32[128,16]{0,1:T(8,128)} async-done(((f32[4096,16]{0,1:T(8,128)}), f32[128,16]{0,1:T(8,128)}) %reduce-scatter.2.cloned.1.call-update) | async-done | bytes 8208 | tf_op jit(solution)/shard_map/reduce_scatter | solution.py:102
  (356 shorter events, 283.3 us)
Async XLA Ops:
  7.2 99.3 %all-gather.2.cloned.1.call-start = ((), (), s32[]{:S(2)}) async-start(), calls=%async_computation.1 | async-start | bytes 4325376 | tf_op jit(solution)/shard_map/all_gather | solution.py:63
  8.2 103.0 %copy-start = (bf16[128,256]{0,1:T(8,128)(2,1)}, bf16[128,256]{0,1:T(8,128)(2,1)S(1)}, u32[]{:S(2)}) copy-start(bf16[128,256]{0,1:T(8,128)(2,1)S(1)} %copy.19) | copy-start | bytes 196612
  9.2 102.0 %copy-start.1 = (bf16[128,256]{0,1:T(8,128)(2,1)}, bf16[128,256]{0,1:T(8,128)(2,1)S(1)}, u32[]{:S(2)}) copy-start(bf16[128,256]{0,1:T(8,128)(2,1)S(1)} %copy.20) | copy-start | bytes 196612
  10.2 101.0 %copy-start.2 = (bf16[128,256]{0,1:T(8,128)(2,1)}, bf16[128,256]{0,1:T(8,128)(2,1)S(1)}, u32[]{:S(2)}) copy-start(bf16[128,256]{0,1:T(8,128)(2,1)S(1)} %copy.21) | copy-start | bytes 196612
  11.1 100.0 %copy-start.3 = (bf16[128,256]{0,1:T(8,128)(2,1)}, bf16[128,256]{0,1:T(8,128)(2,1)S(1)}, u32[]{:S(2)}) copy-start(bf16[128,256]{0,1:T(8,128)(2,1)S(1)} %copy.22) | copy-start | bytes 196612
  11.3 0.6 copy-start.4
  12.6 828.4 %reduce-scatter.2.cloned.1.call-start = ((), (), s32[]{:S(2)}) async-start(), calls=%async_computation.2 | async-start | bytes 270336 | tf_op jit(solution)/shard_map/reduce_scatter | solution.py:102
  69.9 42.0 %copy-start.7 = (s32[16]{0:T(128)S(1)}, s32[16]{0:T(128)}, u32[]{:S(2)}) copy-start(s32[16]{0:T(128)} %param.19) | copy-start | bytes 196
  121.0 1.7 copy-start.5
  135.1 0.9 copy-start.6
Sparse Core Ops, SparseCore 0:
  12.7 93.7 all-gather.1
  395.3 445.6 reduce-scatter.1
